TPU v7x, 32 devices: a whole 2x2x4 slice. The times are simulated.
32 devices in a mesh: groups: 2 (over y), ctx: 4 (over x, core), head: 4 (over z).
Axes of the slice: x: 2, y: 2, z: 4, core: 2. Of those that a mesh axis runs over, the one named last changes fastest.
Arguments:
- queries: bfloat16 [1536, 8, 5, 128], P(('groups', 'ctx'), 'head'), parts along dimension 0, may hold values from -6 to 6
- keys_values: bfloat16 [1536, 8, 2, 128], P(('groups', 'ctx'), 'head'), parts along dimension 0, may hold values from -6 to 6
- prior_state: bfloat16 [16, 8256, 128], P(('groups', 'head'), 'ctx'), parts along dimension 0, may hold values from -224 to 224
- counts: int32 [2], P('groups'), parts along dimension 0, may hold values from 384 to 1535
- continuation: int32 [64], P('groups'), parts along dimension 0, may hold values from 0 to 75967
- query_table: bfloat16 [75968, 8, 5, 128], P('ctx', 'head'), may hold values from -6 to 6
- pair_table: bfloat16 [75968, 8, 2, 128], P('ctx', 'head'), may hold values from -6 to 6
Outputs:
- readout: bfloat16 [1536, 8, 5, 128], P(('groups', 'ctx'), 'head'), parts along dimension 0
- decode_out: bfloat16 [64, 8, 5, 128], P(('groups', 'ctx'), 'head'), parts along dimension 0
- decode_state: float32 [16, 8256, 128], P(('groups', 'head'), 'ctx'), parts along dimension 0
There are 2 independent parts, one for each index of `groups`. A program takes and returns all parts, laid end to end along the dimension named above; an argument that names none is the same for every part. Nothing has to cross between parts.
All inputs are finite; a program needn't handle non-finite values.
Results may differ from a plain program's by a relative error of at most 0.0048.
The roundings to bfloat16 on the way count: a program that leaves them out, or rounds other values in their place, can miss the bound.
Values may be sent and summed in bfloat16 or wider, within the bound.
A program may use at most 256 MiB of HBM per device.

v0:
```python
import functools

import jax
import jax.numpy as jnp
from jax import lax
from jax.experimental import pallas as pl
from jax.experimental.pallas import tpu as pltpu
from jax.sharding import PartitionSpec as P

ROOT_TWO = 2.0**0.5
MESH = pl.DeviceIdType.MESH
TILE = 256
LANES = 128


def round_up(number, multiple):
    return (number + multiple - 1) // multiple * multiple


def pick_kernel(ids_ref, query_table, pair_table, query_out, pair_out, query_sem, pair_sem):
    step_count = query_out.shape[0]

    def copies(step):
        row = ids_ref[step]
        return (
            pltpu.make_async_copy(query_table.at[row], query_out.at[step], query_sem.at[step]),
            pltpu.make_async_copy(pair_table.at[row], pair_out.at[step], pair_sem.at[step]),
        )

    for step in range(step_count):
        for copy in copies(step):
            copy.start()
    for step in range(step_count):
        for copy in copies(step):
            copy.wait()


def pick_rows(ids, query_table, pair_table):
    steps = ids.shape[0]
    return pl.pallas_call(
        pick_kernel,
        out_shape=(
            jax.ShapeDtypeStruct((steps,) + query_table.shape[1:], query_table.dtype),
            jax.ShapeDtypeStruct((steps,) + pair_table.shape[1:], pair_table.dtype),
        ),
        in_specs=[
            pl.BlockSpec(memory_space=pltpu.SMEM),
            pl.BlockSpec(memory_space=pl.ANY),
            pl.BlockSpec(memory_space=pl.ANY),
        ],
        out_specs=(
            pl.BlockSpec(memory_space=pltpu.VMEM),
            pl.BlockSpec(memory_space=pltpu.VMEM),
        ),
        scratch_shapes=[pltpu.SemaphoreType.DMA((steps,)), pltpu.SemaphoreType.DMA((steps,))],
        name="pick_rows",
    )(ids, query_table, pair_table)


def main_kernel(
    sizes,
    queries,
    blob,
    prior,
    out,
    state,
    land_blob,
    land_prior,
    query_rows,
    step_rows,
    key_rows,
    value_rows,
    turned,
    blob_send,
    blob_recv,
    prior_send,
    prior_recv,
    local_sem,
):
    n, heads, group, tok_rows, step_count, rows_valid = sizes
    chips = n // 2
    per_shard = step_count // n
    window_rows = tok_rows * group
    window = n * tok_rows
    prior_rows = prior.shape[1]
    blocks = land_prior.shape[2] // LANES
    row_tiles = out.shape[1] // TILE
    padded_keys = key_rows.shape[1]
    me = lax.axis_index("ctx")
    core = lax.rem(me, 2)
    partner = me + 1 - 2 * core

    def across(step):
        return lax.rem(me + 2 * step, n)

    def twin(index):
        return index + 1 - 2 * lax.rem(index, 2)

    barrier = pltpu.get_barrier_semaphore()
    pl.semaphore_signal(barrier, inc=1, device_id={"ctx": partner}, device_id_type=MESH)
    for step in range(1, chips):
        pl.semaphore_signal(barrier, inc=1, device_id={"ctx": across(step)}, device_id_type=MESH)
    pl.semaphore_wait(barrier, chips)

    def blob_copy(src, source, slot, target):
        return pltpu.make_async_remote_copy(
            src_ref=src,
            dst_ref=land_blob.at[source],
            send_sem=blob_send.at[slot],
            recv_sem=blob_recv.at[source],
            device_id={"ctx": target},
            device_id_type=MESH,
        )

    def prior_copy(src, source, head, slot, target):
        return pltpu.make_async_remote_copy(
            src_ref=src,
            dst_ref=land_prior.at[source, head, pl.ds(0, prior_rows)],
            send_sem=prior_send.at[slot, head],
            recv_sem=prior_recv.at[source, head],
            device_id={"ctx": target},
            device_id_type=MESH,
        )

    def blob_own(slot):
        return blob_copy(blob, me, slot, partner if slot == 0 else across(slot))

    def blob_forward(step):
        source = across(step)
        return blob_copy(land_blob.at[source], source, chips - 1 + step, partner)

    def prior_own(slot, head):
        target = partner if slot == 0 else across(slot)
        return prior_copy(prior.at[head], me, head, slot, target)

    def prior_forward(step, head):
        source = across(step)
        return prior_copy(
            land_prior.at[source, head, pl.ds(0, prior_rows)],
            source,
            head,
            chips - 1 + step,
            partner,
        )

    for slot in list(range(1, chips)) + [0]:
        blob_own(slot).start()
    for head in range(heads):
        for slot in list(range(1, chips)) + [0]:
            prior_own(slot, head).start()
    own_blob = pltpu.make_async_copy(blob, land_blob.at[me], local_sem.at[0])
    own_prior = pltpu.make_async_copy(
        prior, land_prior.at[me, :, pl.ds(0, prior_rows)], local_sem.at[1]
    )
    own_blob.start()
    own_prior.start()

    if prior_rows < blocks * LANES:
        rest = blocks * LANES - prior_rows
        for source in range(n):
            for head in range(heads):
                land_prior[source, head, pl.ds(prior_rows, rest), :] = jnp.zeros(
                    (rest, LANES), jnp.bfloat16
                )
    out[...] = jnp.zeros_like(out)
    for head in range(heads):
        query_rows[head, pl.ds(0, window_rows), :] = queries[head].astype(jnp.float32)
        query_rows[head, pl.ds(window_rows, out.shape[1] - window_rows), :] = jnp.zeros(
            (out.shape[1] - window_rows, LANES), jnp.float32
        )
        spare = padded_keys - window - step_count
        if spare > 0:
            key_rows[head, pl.ds(window + step_count, spare), :] = jnp.zeros(
                (spare, LANES), jnp.bfloat16
            )
            value_rows[head, pl.ds(window + step_count, spare), :] = jnp.zeros(
                (spare, LANES), jnp.bfloat16
            )

    def place(source):
        first = source * rows_valid
        return lax.div(first, LANES), lax.rem(first, LANES)

    def carry_tile(source, head, tile):
        first_offset, lead = place(source)
        rows = pl.ds(pl.multiple_of(tile * TILE, TILE), TILE)
        values = query_rows[head, rows, :]
        scaled = values * ROOT_TWO
        lane = lax.broadcasted_iota(jnp.int32, (TILE, LANES), 1)
        early = lane < LANES - lead

        def turn(array, amount):
            shift = lax.rem(2 * LANES - lax.rem(amount, LANES), LANES)
            return pltpu.roll(array, shift, 1)

        here = turn(values, lead)
        near = turn(scaled, lead + first_offset)
        pieces = []
        for block in range(blocks):
            far = turn(scaled, lead + first_offset + block + 1)
            partner_values = jnp.where(early, near, far)
            if block == 0:
                plain = jnp.logical_and(early, first_offset == 0)
                partner_values = jnp.where(plain, here, partner_values)
            pieces.append((here * partner_values).astype(jnp.bfloat16))
            near = far
        features = jnp.concatenate(pieces, axis=1)
        out[head, rows, :] += jnp.dot(
            features, land_prior[source, head], preferred_element_type=jnp.float32
        )

    def carry(source, head, first_tile, last_tile):
        @pl.loop(first_tile, last_tile)
        def _(tile):
            carry_tile(source, head, tile)

    full_tiles = window_rows // TILE
    own_prior.wait()
    for head in range(heads):
        carry(me, head, 0, full_tiles)

    own_blob.wait()
    blob_copy(blob, partner, 0, partner).wait_recv()
    for step in range(1, chips):
        blob_copy(blob, across(step), 0, partner).wait_recv()
        blob_forward(step).start()
    for step in range(1, chips):
        blob_copy(blob, twin(across(step)), 0, partner).wait_recv()

    for head in range(heads):
        for source in range(n):
            key_rows[head, pl.ds(source * tok_rows, tok_rows), :] = land_blob[
                source, head, pl.ds(0, tok_rows), :
            ]
            value_rows[head, pl.ds(source * tok_rows, tok_rows), :] = land_blob[
                source, heads + head, pl.ds(0, tok_rows), :
            ]

        def picked(plane, first, count):
            total = land_blob[0, plane, pl.ds(first, count), :].astype(jnp.float32)
            for source in range(1, n):
                total += land_blob[source, plane, pl.ds(first, count), :].astype(jnp.float32)
            return total

        key_rows[head, pl.ds(window, step_count), :] = picked(head, tok_rows, step_count).astype(
            jnp.bfloat16
        )
        value_rows[head, pl.ds(window, step_count), :] = picked(
            heads + head, tok_rows, step_count
        ).astype(jnp.bfloat16)
        half = step_count * group // 2
        for side in range(2):
            step_rows[head, pl.ds(side * half, half), :] = picked(
                2 * head + side, tok_rows + step_count, half
            )
        own_steps = per_shard * group
        query_rows[head, pl.ds(window_rows, own_steps), :] = step_rows[
            head, pl.ds(me * own_steps, own_steps), :
        ]

    for head in range(heads):
        carry(me, head, full_tiles, row_tiles)
        prior_copy(prior.at[head], partner, head, 0, partner).wait_recv()
        carry(partner, head, 0, row_tiles)

    first_offset, lead = place(me)
    identity = (
        lax.broadcasted_iota(jnp.int32, (LANES, LANES), 0)
        == lax.broadcasted_iota(jnp.int32, (LANES, LANES), 1)
    ).astype(jnp.bfloat16)
    contract_last = (((1,), (1,)), ((), ()))
    for head in range(heads):
        keys_turned = lax.dot_general(
            identity, key_rows[head], contract_last, preferred_element_type=jnp.float32
        )
        chunks = padded_keys // LANES
        for chunk in range(chunks):
            piece = keys_turned[:, chunk * LANES : (chunk + 1) * LANES]
            turned[head, chunk, pl.ds(0, LANES), :] = piece
            turned[head, chunk, pl.ds(LANES, LANES), :] = piece

        def state_block(block):
            row = lax.broadcasted_iota(jnp.int32, (LANES, LANES), 0)
            early = row < LANES - lead
            plain = jnp.logical_and(early, first_offset + block == 0)
            factor = jnp.where(plain, 1.0, ROOT_TWO)
            near_row = lax.rem(lead + first_offset + block, LANES)
            far_row = lax.rem(lead + first_offset + block + 1, LANES)
            pieces = []
            for chunk in range(chunks):
                here = turned[head, chunk, pl.ds(lead, LANES), :]
                near = turned[head, chunk, pl.ds(near_row, LANES), :]
                far = turned[head, chunk, pl.ds(far_row, LANES), :]
                both = jnp.where(early, near, far) * factor
                pieces.append((here * both).astype(jnp.bfloat16))
            features = jnp.concatenate(pieces, axis=1)
            return jnp.dot(features, value_rows[head], preferred_element_type=jnp.float32)

        whole_blocks = prior_rows // LANES

        @pl.loop(0, whole_blocks)
        def _(block):
            state[head, pl.ds(pl.multiple_of(block * LANES, LANES), LANES), :] = state_block(block)

        rest = prior_rows - whole_blocks * LANES
        if rest > 0:
            state[head, pl.ds(whole_blocks * LANES, rest), :] = state_block(whole_blocks)[:rest]

        @pl.loop(0, row_tiles)
        def _(tile):
            rows = pl.ds(pl.multiple_of(tile * TILE, TILE), TILE)
            scores = lax.dot_general(
                query_rows[head, rows, :].astype(jnp.bfloat16),
                key_rows[head],
                contract_last,
                preferred_element_type=jnp.float32,
            )
            local = tile * TILE + lax.broadcasted_iota(jnp.int32, (TILE, 1), 0)
            position = jnp.where(
                local < window_rows,
                local + me * window_rows,
                local - window_rows + window * group + me * (per_shard * group),
            )
            key_index = lax.broadcasted_iota(jnp.int32, scores.shape, 1)
            allowed = position >= key_index * group
            weights = jnp.where(allowed, scores * scores, 0.0).astype(jnp.bfloat16)
            out[head, rows, :] += jnp.dot(
                weights, value_rows[head], preferred_element_type=jnp.float32
            )

    for step in range(1, chips):
        source = across(step)
        for head in range(heads):
            prior_copy(prior.at[head], source, head, 0, partner).wait_recv()
            prior_forward(step, head).start()
            carry(source, head, 0, row_tiles)
            prior_copy(prior.at[head], twin(source), head, 0, partner).wait_recv()
            carry(twin(source), head, 0, row_tiles)

    for slot in range(chips):
        blob_own(slot).wait_send()
        for head in range(heads):
            prior_own(slot, head).wait_send()
    for step in range(1, chips):
        blob_forward(step).wait_send()
        for head in range(heads):
            prior_forward(step, head).wait_send()


def combine(sizes, queries, blob, prior, out_rows):
    n, heads, group, tok_rows, step_count, rows_valid = sizes
    prior_rows = prior.shape[1]
    padded_rows = round_up(prior_rows, LANES)
    padded_keys = round_up(n * tok_rows + step_count, LANES)
    slots = 2 * (n // 2) - 1
    vmem = pl.BlockSpec(memory_space=pltpu.VMEM)
    return pl.pallas_call(
        functools.partial(main_kernel, sizes),
        out_shape=(
            jax.ShapeDtypeStruct((heads, out_rows, LANES), jnp.float32),
            jax.ShapeDtypeStruct((heads, prior_rows, LANES), jnp.float32),
        ),
        in_specs=[vmem] * 3,
        out_specs=(vmem, vmem),
        scratch_shapes=[
            pltpu.VMEM((n,) + blob.shape, jnp.bfloat16),
            pltpu.VMEM((n, heads, padded_rows, LANES), jnp.bfloat16),
            pltpu.VMEM((heads, out_rows, LANES), jnp.float32),
            pltpu.VMEM((heads, step_count * group, LANES), jnp.float32),
            pltpu.VMEM((heads, padded_keys, LANES), jnp.bfloat16),
            pltpu.VMEM((heads, padded_keys, LANES), jnp.bfloat16),
            pltpu.VMEM((heads, padded_keys // LANES, 2 * LANES, LANES), jnp.float32),
            pltpu.SemaphoreType.DMA((slots,)),
            pltpu.SemaphoreType.DMA((n,)),
            pltpu.SemaphoreType.DMA((slots, heads)),
            pltpu.SemaphoreType.DMA((n, heads)),
            pltpu.SemaphoreType.DMA((2,)),
        ],
        compiler_params=pltpu.CompilerParams(
            collective_id=0, has_side_effects=True, vmem_limit_bytes=56 * 2**20
        ),
        name="combine",
    )(queries, blob, prior)


def on_device(queries, keys_values, prior_state, counts, continuation, query_table, pair_table):
    tok_rows, heads, group, head_size = queries.shape
    n = lax.axis_size("ctx")
    shard_index = lax.axis_index("ctx")
    step_count = continuation.shape[0]
    per_shard = step_count // n
    rows_valid = prior_state.shape[1]

    vocab_rows = query_table.shape[0]
    local_ids = continuation - shard_index * vocab_rows
    inside = (local_ids >= 0) & (local_ids < vocab_rows)
    safe_ids = jnp.clip(local_ids, 0, vocab_rows - 1)
    query_pick, pair_pick = pick_rows(safe_ids, query_table.transpose(0, 2, 1, 3), pair_table)
    mask = inside[:, None, None, None]
    query_pick = jnp.where(mask, query_pick, jnp.zeros_like(query_pick))
    pair_pick = jnp.where(mask, pair_pick, jnp.zeros_like(pair_pick))

    window_planes = keys_values.transpose(2, 1, 0, 3).reshape(2 * heads, tok_rows, head_size)
    step_planes = pair_pick.transpose(2, 1, 0, 3)
    step_planes = step_planes.reshape(2 * heads, step_count, head_size)
    query_planes = query_pick.transpose(2, 0, 1, 3).reshape(
        2 * heads, step_count * group // 2, head_size
    )
    blob = jnp.concatenate([window_planes, step_planes, query_planes], axis=1)
    query_planes = queries.transpose(1, 0, 2, 3).reshape(heads, tok_rows * group, head_size)
    prior_rows = round_up(rows_valid, 16)
    prior = prior_state
    if prior_rows > rows_valid:
        prior = jnp.pad(prior_state, ((0, 0), (0, prior_rows - rows_valid), (0, 0)))
    out_rows = round_up((tok_rows + per_shard) * group, TILE)
    sizes = (n, heads, group, tok_rows, step_count, rows_valid)
    total, added = combine(sizes, query_planes, blob, prior, out_rows)

    decode_state = prior_state.astype(jnp.float32) + added[:, :rows_valid]

    def finish(rows, first_position):
        count = rows.shape[1] // group
        positions = first_position + jnp.arange(count, dtype=jnp.int32) + 1
        scale = 1.0 / (head_size * jnp.sqrt(positions.astype(jnp.float32)))
        rows = rows.reshape(heads, count, group, head_size) * scale[None, :, None, None]
        return rows.astype(jnp.bfloat16).transpose(1, 0, 2, 3)

    window_rows = tok_rows * group
    readout = finish(total[:, :window_rows], counts[0] + shard_index * tok_rows)
    decode_out = finish(
        total[:, window_rows : window_rows + per_shard * group],
        counts[0] + n * tok_rows + shard_index * per_shard,
    )
    return (readout, decode_out, decode_state)


def solution(mesh):
    in_specs = (
        P(("groups", "ctx"), "head", None, None),
        P(("groups", "ctx"), "head", None, None),
        P(("groups", "head"), "ctx", None),
        P("groups"),
        P("groups"),
        P("ctx", "head", None, None),
        P("ctx", "head", None, None),
    )
    out_specs = (
        P(("groups", "ctx"), "head", None, None),
        P(("groups", "ctx"), "head", None, None),
        P(("groups", "head"), "ctx", None),
    )
    return jax.shard_map(
        on_device, mesh=mesh, in_specs=in_specs, out_specs=out_specs, check_vma=False
    )
```

profile of v0, /device:TPU:1, one launch (start us, length us, event | category | flops | bytes accessed | tf_op | source)
XLA Modules:
  0.0 67.9 jit_solution(11153295715503110439)
XLA Ops:
  0.6 1.2 %subtract_clamp_fusion.ids_ref = s32[32]{0:T(128)} fusion(s32[32]{0:T(128)} %param.11, s32[]{:T(128)S(6)} %mul.42), kind=kLoop, calls=%fused_computation.13 | loop fusion | flops 64 | bytes 260 | tf_op jit(solution)/shard_map/jit(clip)/min | solution.py:397
  1.8 0.0 copy-start.3
  1.8 0.0 copy-start.2
  1.8 0.0 copy-start.1
  1.8 3.4 %pick_rows.1 = (bf16[32,5,2,128]{3,2,1,0:T(2,128)(2,1)}, bf16[32,2,2,128]{3,2,1,0:T(2,128)(2,1)}) custom-call(s32[32]{0:T(128)} %subtract_clamp_fusion.ids_ref, bf16[18992,5,2,128]{3,2,1,0:T(2,128)(2,1)} %bitcast.20, bf16[18992,2,2,128]{3,2,1,0:T(2,128)(2,1)} %pair_table.1), custom_call_target="tpu_custom_call" | custom-call | tf_op jit(solution)/shard_map/pick_rows/pallas_call | solution.py:40
  5.2 0.0 copy-done.3
  5.3 1.0 %fusion.1 = bf16[2,32,5,128]{3,0,2,1:T(2,128)(2,1)S(1)} fusion(bf16[32,5,2,128]{3,2,1,0:T(2,128)(2,1)} %get-tuple-element.8, pred[32]{0:T(512)(128)(4,1)S(1)} %compare_and_fusion), kind=kLoop, calls=%fused_computation.5 | loop fusion | flops 40960 | bytes 163872 | tf_op jit(solution)/shard_map/transpose | solution.py:406
  6.4 0.9 %fusion.2 = bf16[2,2,32,128]{3,0,1,2:T(2,128)(2,1)S(1)} fusion(bf16[32,2,2,128]{3,2,1,0:T(2,128)(2,1)} %get-tuple-element.7, pred[32]{0:T(512)(128)(4,1)S(1)} %compare_and_fusion), kind=kLoop, calls=%fused_computation.8 | loop fusion | flops 16384 | bytes 65568 | tf_op jit(solution)/shard_map/transpose | solution.py:404
  7.3 0.0 copy-done.2
  7.3 0.7 %pad_maximum_fusion.blob = bf16[4,304,128]{2,1,0:T(8,128)(2,1)} fusion(bf16[4,80,128]{2,1,0:T(8,128)(2,1)S(1)} %reshape.46, bf16[4,32,128]{2,1,0:T(8,128)(2,1)S(1)} %bitcast.26, bf16[4,192,128]{2,1,0:T(8,128)(2,1)S(1)} %bitcast.22), kind=kLoop, calls=%fused_computation.3 | loop fusion | flops 933888 | bytes 622592 | tf_op jit(solution)/shard_map/concatenate | solution.py:409
  8.1 0.0 copy-done.1
  8.1 0.8 %copy.19.queries = bf16[2,960,128]{2,1,0:T(8,128)(2,1)} copy(bf16[2,960,128]{2,0,1:T(2,128)(2,1)S(1)} %bitcast.23) | data formatting | bytes 983040 | tf_op jit(solution)/shard_map/reshape | solution.py:410
  8.9 50.5 %combine.1 = (f32[2,1024,128]{2,1,0:T(8,128)}, f32[2,2064,128]{2,1,0:T(8,128)}) custom-call(bf16[2,960,128]{2,1,0:T(8,128)(2,1)} %copy.19.queries, bf16[4,304,128]{2,1,0:T(8,128)(2,1)} %pad_maximum_fusion.blob, bf16[2,2064,128]{2,1,0:T(8,128)(2,1)} %prior.1), custom_call_target="tpu_custom_call" | custom-call | tf_op jit(solution)/shard_map/combine/pallas_call | solution.py:357
  59.4 1.3 %slice.6 = f32[2,960,128]{2,1,0:T(8,128)S(1)} slice(f32[2,1024,128]{2,1,0:T(8,128)} %get-tuple-element.9), slice={[0:2], [0:960], [0:128]} | slice | bytes 1966080 | tf_op jit(solution)/shard_map/slice | solution.py:429
  60.7 0.0 copy-start
  60.7 0.8 %copy.20 = f32[2,960,128]{2,0,1:T(2,128)S(1)} copy(f32[2,960,128]{2,1,0:T(8,128)S(1)} %slice.6) | data formatting | bytes 1966080 | tf_op jit(solution)/shard_map/slice | solution.py:429
  62.1 1.2 %fusion = bf16[192,2,5,128]{3,1,2,0:T(2,128)(2,1)} fusion(f32[2,192,5,128]{3,0,2,1:T(2,128)S(1)} %bitcast.21, f32[192]{0:T(256)S(1)} %multiply_divide_fusion), kind=kLoop, calls=%fused_computation.2 | loop fusion | flops 491520 | bytes 1475328 | tf_op jit(solution)/shard_map/transpose | solution.py:426
  63.3 0.8 %slice.7 = f32[2,40,128]{2,1,0:T(8,128)S(1)} slice(f32[2,1024,128]{2,1,0:T(8,128)} %get-tuple-element.9), slice={[0:2], [960:1000], [0:128]} | slice | bytes 81920 | tf_op jit(solution)/shard_map/slice | solution.py:431
  64.1 0.7 %fusion.3 = bf16[8,2,5,128]{3,1,2,0:T(2,128)(2,1)} fusion(f32[2,8,5,128]{3,0,2,1:T(2,128)S(1)} %bitcast.25, f32[8]{0:T(128)S(1)} %multiply_divide_fusion.1), kind=kLoop, calls=%fused_computation.9 | loop fusion | flops 20480 | bytes 61472 | tf_op jit(solution)/shard_map/transpose | solution.py:426
  64.8 0.0 copy-done
  64.8 3.1 %convert_add_fusion = f32[2,2064,128]{2,1,0:T(8,128)} fusion(f32[2,2064,128]{2,1,0:T(8,128)} %get-tuple-element.10, bf16[2,2064,128]{2,1,0:T(8,128)(2,1)S(1)} %copy-done), kind=kLoop, calls=%fused_computation | loop fusion | flops 1056768 | bytes 5283840 | tf_op jit(solution)/shard_map/add | solution.py:419
  (8 shorter events, 0.2 us)
Async XLA Ops:
  1.8 3.4 %copy-start.3 = (s32[32]{0:T(128)S(1)}, s32[32]{0:T(128)}, u32[]{:S(2)}) copy-start(s32[32]{0:T(128)} %param.11) | copy-start | bytes 388
  1.8 5.5 %copy-start.2 = (bf16[192,2,2,128]{3,2,1,0:T(2,128)(2,1)S(1)}, bf16[192,2,2,128]{3,2,1,0:T(2,128)(2,1)}, u32[]{:S(2)}) copy-start(bf16[192,2,2,128]{3,2,1,0:T(2,128)(2,1)} %param.8) | copy-start | bytes 589828
  1.8 6.3 %copy-start.1 = (bf16[192,2,5,128]{3,1,2,0:T(2,128)(2,1)S(1)}, bf16[192,2,5,128]{3,1,2,0:T(2,128)(2,1)}, u32[]{:S(2)}) copy-start(bf16[192,2,5,128]{3,1,2,0:T(2,128)(2,1)} %param.7) | copy-start | bytes 1474564
  60.7 4.2 %copy-start = (bf16[2,2064,128]{2,1,0:T(8,128)(2,1)S(1)}, bf16[2,2064,128]{2,1,0:T(8,128)(2,1)}, u32[]{:S(2)}) copy-start(bf16[2,2064,128]{2,1,0:T(8,128)(2,1)} %prior.1) | copy-start | bytes 3170308
where the time goes:
time: 68.4 us; the launch traced here: 67.9 us
  Pallas kernels  53.9 us (79%)
  other arithmetic  8.85 us (13%)
  local copies, waits for them, and re-layouts  3.8 us (6%)
  between operations  1.41 us (2%)
    pallas_call x1, Pallas kernels, combine(): pl.pallas_call(functools.partial(main_kernel, sizes), out_shape=(jax.Shap...  50.5 us
    pallas_call x1, Pallas kernels, pick_rows(): pl.pallas_call(pick_kernel, out_shape=(jax.ShapeDtypeStruct((steps,) + qu...  3.41 us
    add x1, other arithmetic, on_device(): decode_state = prior_state.astype(jnp.float32) + added[:, :rows_valid]  3.09 us
    slice x2, local copies, waits for them, and re-layouts, on_device(): readout = finish(total[:, :window_rows], counts[0] + shard_index * tok_rows)  2.03 us
    transpose x2, other arithmetic, finish(): return rows.astype(jnp.bfloat16).transpose(1, 0, 2, 3)  1.9 us

commit v1 on v0

--- a/solution.py
+++ b/solution.py
@@ -67,6 +67,10 @@
     land_blob,
     land_prior,
     query_rows,
+    query_plain,
+    query_scaled,
+    prior_turned,
+    total_turned,
     step_rows,
     key_rows,
     value_rows,
@@ -83,6 +87,8 @@
     window_rows = tok_rows * group
     window = n * tok_rows
     prior_rows = prior.shape[1]
+    shifted = prior_rows == rows_valid
+    state_rows = state.shape[1]
     blocks = land_prior.shape[2] // LANES
     row_tiles = out.shape[1] // TILE
     padded_keys = key_rows.shape[1]
@@ -112,10 +118,14 @@
             device_id_type=MESH,
         )
 
+    def landing(source):
+        first = pl.multiple_of(lax.rem(source * rows_valid, LANES), 16) if shifted else 0
+        return pl.ds(first, prior_rows)
+
     def prior_copy(src, source, head, slot, target):
         return pltpu.make_async_remote_copy(
             src_ref=src,
-            dst_ref=land_prior.at[source, head, pl.ds(0, prior_rows)],
+            dst_ref=land_prior.at[source, head, landing(source)],
             send_sem=prior_send.at[slot, head],
             recv_sem=prior_recv.at[source, head],
             device_id={"ctx": target},
@@ -136,7 +146,7 @@
     def prior_forward(step, head):
         source = across(step)
         return prior_copy(
-            land_prior.at[source, head, pl.ds(0, prior_rows)],
+            land_prior.at[source, head, landing(source)],
             source,
             head,
             chips - 1 + step,
@@ -150,23 +160,28 @@
             prior_own(slot, head).start()
     own_blob = pltpu.make_async_copy(blob, land_blob.at[me], local_sem.at[0])
     own_prior = pltpu.make_async_copy(
-        prior, land_prior.at[me, :, pl.ds(0, prior_rows)], local_sem.at[1]
+        prior, land_prior.at[me, :, landing(me)], local_sem.at[1]
     )
     own_blob.start()
     own_prior.start()
 
-    if prior_rows < blocks * LANES:
-        rest = blocks * LANES - prior_rows
+    if shifted:
         for source in range(n):
-            for head in range(heads):
-                land_prior[source, head, pl.ds(prior_rows, rest), :] = jnp.zeros(
-                    (rest, LANES), jnp.bfloat16
-                )
-    out[...] = jnp.zeros_like(out)
-    for head in range(heads):
-        query_rows[head, pl.ds(0, window_rows), :] = queries[head].astype(jnp.float32)
+            lead_rows = source * rows_valid % LANES
+            for first, last in (
+                (0, lead_rows),
+                (lead_rows + prior_rows, blocks * LANES),
+            ):
+                if last > first:
+                    for head in range(heads):
+                        land_prior[source, head, pl.ds(first, last - first), :] = jnp.zeros(
+                            (last - first, LANES), jnp.bfloat16
+                        )
+    total_turned[...] = jnp.zeros_like(total_turned)
+    for head in range(heads):
+        query_rows[head, pl.ds(0, window_rows), :] = queries[head]
         query_rows[head, pl.ds(window_rows, out.shape[1] - window_rows), :] = jnp.zeros(
-            (out.shape[1] - window_rows, LANES), jnp.float32
+            (out.shape[1] - window_rows, LANES), jnp.bfloat16
         )
         spare = padded_keys - window - step_count
         if spare > 0:
@@ -181,35 +196,47 @@
         first = source * rows_valid
         return lax.div(first, LANES), lax.rem(first, LANES)
 
+    identity = (
+        lax.broadcasted_iota(jnp.int32, (LANES, LANES), 0)
+        == lax.broadcasted_iota(jnp.int32, (LANES, LANES), 1)
+    ).astype(jnp.bfloat16)
+    contract_last = (((1,), (1,)), ((), ()))
+
+    def transposed(rows):
+        return lax.dot_general(identity, rows, contract_last, preferred_element_type=jnp.float32)
+
+    chunks_per_tile = TILE // LANES
+
+    def turn_queries(head, first_tile, last_tile):
+        for chunk in range(first_tile * chunks_per_tile, last_tile * chunks_per_tile):
+            piece = transposed(query_rows[head, pl.ds(chunk * LANES, LANES), :])
+            scaled = piece * ROOT_TWO
+            query_plain[head, chunk] = piece
+            query_scaled[head, chunk, pl.ds(0, LANES), :] = scaled
+            query_scaled[head, chunk, pl.ds(LANES, LANES), :] = scaled
+
     def carry_tile(source, head, tile):
-        first_offset, lead = place(source)
-        rows = pl.ds(pl.multiple_of(tile * TILE, TILE), TILE)
-        values = query_rows[head, rows, :]
-        scaled = values * ROOT_TWO
-        lane = lax.broadcasted_iota(jnp.int32, (TILE, LANES), 1)
-        early = lane < LANES - lead
-
-        def turn(array, amount):
-            shift = lax.rem(2 * LANES - lax.rem(amount, LANES), LANES)
-            return pltpu.roll(array, shift, 1)
-
-        here = turn(values, lead)
-        near = turn(scaled, lead + first_offset)
-        pieces = []
-        for block in range(blocks):
-            far = turn(scaled, lead + first_offset + block + 1)
-            partner_values = jnp.where(early, near, far)
-            if block == 0:
-                plain = jnp.logical_and(early, first_offset == 0)
-                partner_values = jnp.where(plain, here, partner_values)
-            pieces.append((here * partner_values).astype(jnp.bfloat16))
-            near = far
-        features = jnp.concatenate(pieces, axis=1)
-        out[head, rows, :] += jnp.dot(
-            features, land_prior[source, head], preferred_element_type=jnp.float32
+        first_offset, _ = place(source)
+        columns = []
+        for side in range(chunks_per_tile):
+            chunk = tile * chunks_per_tile + side
+            here = query_plain[head, chunk]
+            pieces = []
+            for block in range(blocks):
+                row = lax.rem(first_offset + block, LANES)
+                other = query_scaled[head, chunk, pl.ds(row, LANES), :]
+                if block == 0:
+                    other = jnp.where(first_offset == 0, here, other)
+                pieces.append((here * other).astype(jnp.bfloat16))
+            columns.append(jnp.concatenate(pieces, axis=0))
+        features = jnp.concatenate(columns, axis=1)
+        total_turned[head, tile] += jnp.dot(
+            prior_turned[...], features, preferred_element_type=jnp.float32
         )
 
     def carry(source, head, first_tile, last_tile):
+        prior_turned[...] = transposed(land_prior[source, head]).astype(jnp.bfloat16)
+
         @pl.loop(first_tile, last_tile)
         def _(tile):
             carry_tile(source, head, tile)
@@ -217,6 +244,7 @@
     full_tiles = window_rows // TILE
     own_prior.wait()
     for head in range(heads):
+        turn_queries(head, 0, full_tiles)
         carry(me, head, 0, full_tiles)
 
     own_blob.wait()
@@ -254,9 +282,9 @@
                 2 * head + side, tok_rows + step_count, half
             )
         own_steps = per_shard * group
-        query_rows[head, pl.ds(window_rows, own_steps), :] = step_rows[
-            head, pl.ds(me * own_steps, own_steps), :
-        ]
+        own_rows = step_rows[head, pl.ds(me * own_steps, own_steps), :]
+        query_rows[head, pl.ds(window_rows, own_steps), :] = own_rows.astype(jnp.bfloat16)
+        turn_queries(head, full_tiles, row_tiles)
 
     for head in range(heads):
         carry(me, head, full_tiles, row_tiles)
@@ -264,15 +292,8 @@
         carry(partner, head, 0, row_tiles)
 
     first_offset, lead = place(me)
-    identity = (
-        lax.broadcasted_iota(jnp.int32, (LANES, LANES), 0)
-        == lax.broadcasted_iota(jnp.int32, (LANES, LANES), 1)
-    ).astype(jnp.bfloat16)
-    contract_last = (((1,), (1,)), ((), ()))
-    for head in range(heads):
-        keys_turned = lax.dot_general(
-            identity, key_rows[head], contract_last, preferred_element_type=jnp.float32
-        )
+    for head in range(heads):
+        keys_turned = transposed(key_rows[head])
         chunks = padded_keys // LANES
         for chunk in range(chunks):
             piece = keys_turned[:, chunk * LANES : (chunk + 1) * LANES]
@@ -296,13 +317,13 @@
             features = jnp.concatenate(pieces, axis=1)
             return jnp.dot(features, value_rows[head], preferred_element_type=jnp.float32)
 
-        whole_blocks = prior_rows // LANES
+        whole_blocks = state_rows // LANES
 
         @pl.loop(0, whole_blocks)
         def _(block):
             state[head, pl.ds(pl.multiple_of(block * LANES, LANES), LANES), :] = state_block(block)
 
-        rest = prior_rows - whole_blocks * LANES
+        rest = state_rows - whole_blocks * LANES
         if rest > 0:
             state[head, pl.ds(whole_blocks * LANES, rest), :] = state_block(whole_blocks)[:rest]
 
@@ -310,7 +331,7 @@
         def _(tile):
             rows = pl.ds(pl.multiple_of(tile * TILE, TILE), TILE)
             scores = lax.dot_general(
-                query_rows[head, rows, :].astype(jnp.bfloat16),
+                query_rows[head, rows, :],
                 key_rows[head],
                 contract_last,
                 preferred_element_type=jnp.float32,
@@ -324,7 +345,7 @@
             key_index = lax.broadcasted_iota(jnp.int32, scores.shape, 1)
             allowed = position >= key_index * group
             weights = jnp.where(allowed, scores * scores, 0.0).astype(jnp.bfloat16)
-            out[head, rows, :] += jnp.dot(
+            out[head, rows, :] = jnp.dot(
                 weights, value_rows[head], preferred_element_type=jnp.float32
             )
 
@@ -337,6 +358,10 @@
             prior_copy(prior.at[head], twin(source), head, 0, partner).wait_recv()
             carry(twin(source), head, 0, row_tiles)
 
+    for head in range(heads):
+        for tile in range(row_tiles):
+            out[head, pl.ds(tile * TILE, TILE), :] += total_turned[head, tile].T
+
     for slot in range(chips):
         blob_own(slot).wait_send()
         for head in range(heads):
@@ -349,8 +374,10 @@
 
 def combine(sizes, queries, blob, prior, out_rows):
     n, heads, group, tok_rows, step_count, rows_valid = sizes
-    prior_rows = prior.shape[1]
-    padded_rows = round_up(prior_rows, LANES)
+    lead = max(source * rows_valid % LANES for source in range(n))
+    padded_rows = round_up(lead + rows_valid, LANES)
+    chunks = out_rows // LANES
+    state_rows = round_up(rows_valid, 8)
     padded_keys = round_up(n * tok_rows + step_count, LANES)
     slots = 2 * (n // 2) - 1
     vmem = pl.BlockSpec(memory_space=pltpu.VMEM)
@@ -358,14 +385,18 @@
         functools.partial(main_kernel, sizes),
         out_shape=(
             jax.ShapeDtypeStruct((heads, out_rows, LANES), jnp.float32),
-            jax.ShapeDtypeStruct((heads, prior_rows, LANES), jnp.float32),
+            jax.ShapeDtypeStruct((heads, state_rows, LANES), jnp.float32),
         ),
         in_specs=[vmem] * 3,
         out_specs=(vmem, vmem),
         scratch_shapes=[
             pltpu.VMEM((n,) + blob.shape, jnp.bfloat16),
             pltpu.VMEM((n, heads, padded_rows, LANES), jnp.bfloat16),
-            pltpu.VMEM((heads, out_rows, LANES), jnp.float32),
+            pltpu.VMEM((heads, out_rows, LANES), jnp.bfloat16),
+            pltpu.VMEM((heads, chunks, LANES, LANES), jnp.float32),
+            pltpu.VMEM((heads, chunks, 2 * LANES, LANES), jnp.float32),
+            pltpu.VMEM((LANES, padded_rows), jnp.bfloat16),
+            pltpu.VMEM((heads, out_rows // TILE, LANES, TILE), jnp.float32),
             pltpu.VMEM((heads, step_count * group, LANES), jnp.float32),
             pltpu.VMEM((heads, padded_keys, LANES), jnp.bfloat16),
             pltpu.VMEM((heads, padded_keys, LANES), jnp.bfloat16),
@@ -408,10 +439,14 @@
     )
     blob = jnp.concatenate([window_planes, step_planes, query_planes], axis=1)
     query_planes = queries.transpose(1, 0, 2, 3).reshape(heads, tok_rows * group, head_size)
-    prior_rows = round_up(rows_valid, 16)
     prior = prior_state
-    if prior_rows > rows_valid:
-        prior = jnp.pad(prior_state, ((0, 0), (0, prior_rows - rows_valid), (0, 0)))
+    if rows_valid % 16 != 0:
+        leads = [source * rows_valid % LANES for source in range(n)]
+        prior = lax.dynamic_update_slice(
+            jnp.zeros((heads, round_up(max(leads) + rows_valid, LANES), LANES), prior.dtype),
+            prior_state,
+            (0, shard_index * rows_valid % LANES, 0),
+        )
     out_rows = round_up((tok_rows + per_shard) * group, TILE)
     sizes = (n, heads, group, tok_rows, step_count, rows_valid)
     total, added = combine(sizes, query_planes, blob, prior, out_rows)

time: 68.4 us -> 60 us (0.88)
  Pallas kernels: 53.9 us -> 45.5 us
    pallas_call x1, Pallas kernels: 50.5 us -> 42 us  [combine(): pl.pallas_call(functools.partial(main_kernel, sizes), out_shape=(jax.Shap...]
where the time goes in v1:
time: 60 us; the launch traced here: 59.5 us
  Pallas kernels  45.5 us (76%)
  other arithmetic  8.85 us (15%)
  local copies, waits for them, and re-layouts  3.8 us (6%)
  between operations  1.41 us (2%)
    pallas_call x1, Pallas kernels, combine(): pl.pallas_call(functools.partial(main_kernel, sizes), out_shape=(jax.Shap...  42 us
    pallas_call x1, Pallas kernels, pick_rows(): pl.pallas_call(pick_kernel, out_shape=(jax.ShapeDtypeStruct((steps,) + qu...  3.45 us
    add x1, other arithmetic, on_device(): decode_state = prior_state.astype(jnp.float32) + added[:, :rows_valid]  3.09 us
    slice x2, local copies, waits for them, and re-layouts, on_device(): readout = finish(total[:, :window_rows], counts[0] + shard_index * tok_rows)  2.03 us
    transpose x2, other arithmetic, finish(): return rows.astype(jnp.bfloat16).transpose(1, 0, 2, 3)  1.9 us

profile of v1, /device:TPU:1, one launch (start us, length us, event | category | flops | bytes accessed | tf_op | source)
XLA Modules:
  0.0 59.5 jit_solution(7168001507347419326)
XLA Ops:
  0.6 1.2 %subtract_clamp_fusion.ids_ref = s32[32]{0:T(128)} fusion(s32[32]{0:T(128)} %param.11, s32[]{:T(128)S(6)} %mul.42), kind=kLoop, calls=%fused_computation.13 | loop fusion | flops 64 | bytes 260 | tf_op jit(solution)/shard_map/jit(clip)/min | solution.py:428
  1.8 0.0 copy-start.3
  1.8 0.0 copy-start.2
  1.8 0.0 copy-start.1
  1.8 3.4 %pick_rows.1 = (bf16[32,5,2,128]{3,2,1,0:T(2,128)(2,1)}, bf16[32,2,2,128]{3,2,1,0:T(2,128)(2,1)}) custom-call(s32[32]{0:T(128)} %subtract_clamp_fusion.ids_ref, bf16[18992,5,2,128]{3,2,1,0:T(2,128)(2,1)} %bitcast.20, bf16[18992,2,2,128]{3,2,1,0:T(2,128)(2,1)} %pair_table.1), custom_call_target="tpu_custom_call" | custom-call | tf_op jit(solution)/shard_map/pick_rows/pallas_call | solution.py:40
  5.3 0.0 copy-done.3
  5.3 1.0 %fusion.1 = bf16[2,32,5,128]{3,0,2,1:T(2,128)(2,1)S(1)} fusion(bf16[32,5,2,128]{3,2,1,0:T(2,128)(2,1)} %get-tuple-element.8, pred[32]{0:T(512)(128)(4,1)S(1)} %compare_and_fusion), kind=kLoop, calls=%fused_computation.5 | loop fusion | flops 40960 | bytes 163872 | tf_op jit(solution)/shard_map/transpose | solution.py:437
  6.4 0.9 %fusion.2 = bf16[2,2,32,128]{3,0,1,2:T(2,128)(2,1)S(1)} fusion(bf16[32,2,2,128]{3,2,1,0:T(2,128)(2,1)} %get-tuple-element.7, pred[32]{0:T(512)(128)(4,1)S(1)} %compare_and_fusion), kind=kLoop, calls=%fused_computation.8 | loop fusion | flops 16384 | bytes 65568 | tf_op jit(solution)/shard_map/transpose | solution.py:435
  7.3 0.0 copy-done.2
  7.4 0.7 %pad_maximum_fusion.blob = bf16[4,304,128]{2,1,0:T(8,128)(2,1)} fusion(bf16[4,80,128]{2,1,0:T(8,128)(2,1)S(1)} %reshape.46, bf16[4,32,128]{2,1,0:T(8,128)(2,1)S(1)} %bitcast.26, bf16[4,192,128]{2,1,0:T(8,128)(2,1)S(1)} %bitcast.22), kind=kLoop, calls=%fused_computation.3 | loop fusion | flops 933888 | bytes 622592 | tf_op jit(solution)/shard_map/concatenate | solution.py:440
  8.1 0.0 copy-done.1
  8.1 0.8 %copy.19.queries = bf16[2,960,128]{2,1,0:T(8,128)(2,1)} copy(bf16[2,960,128]{2,0,1:T(2,128)(2,1)S(1)} %bitcast.23) | data formatting | bytes 983040 | tf_op jit(solution)/shard_map/reshape | solution.py:441
  8.9 42.0 %combine.1 = (f32[2,1024,128]{2,1,0:T(8,128)}, f32[2,2064,128]{2,1,0:T(8,128)}) custom-call(bf16[2,960,128]{2,1,0:T(8,128)(2,1)} %copy.19.queries, bf16[4,304,128]{2,1,0:T(8,128)(2,1)} %pad_maximum_fusion.blob, bf16[2,2064,128]{2,1,0:T(8,128)(2,1)} %prior.1), custom_call_target="tpu_custom_call" | custom-call | tf_op jit(solution)/shard_map/combine/pallas_call | solution.py:384
  51.0 1.3 %slice.6 = f32[2,960,128]{2,1,0:T(8,128)S(1)} slice(f32[2,1024,128]{2,1,0:T(8,128)} %get-tuple-element.9), slice={[0:2], [0:960], [0:128]} | slice | bytes 1966080 | tf_op jit(solution)/shard_map/slice | solution.py:464
  52.2 0.0 copy-start
  52.3 0.8 %copy.20 = f32[2,960,128]{2,0,1:T(2,128)S(1)} copy(f32[2,960,128]{2,1,0:T(8,128)S(1)} %slice.6) | data formatting | bytes 1966080 | tf_op jit(solution)/shard_map/slice | solution.py:464
  53.7 1.2 %fusion = bf16[192,2,5,128]{3,1,2,0:T(2,128)(2,1)} fusion(f32[2,192,5,128]{3,0,2,1:T(2,128)S(1)} %bitcast.21, f32[192]{0:T(256)S(1)} %multiply_divide_fusion), kind=kLoop, calls=%fused_computation.2 | loop fusion | flops 491520 | bytes 1475328 | tf_op jit(solution)/shard_map/transpose | solution.py:461
  54.9 0.8 %slice.7 = f32[2,40,128]{2,1,0:T(8,128)S(1)} slice(f32[2,1024,128]{2,1,0:T(8,128)} %get-tuple-element.9), slice={[0:2], [960:1000], [0:128]} | slice | bytes 81920 | tf_op jit(solution)/shard_map/slice | solution.py:466
  55.7 0.7 %fusion.3 = bf16[8,2,5,128]{3,1,2,0:T(2,128)(2,1)} fusion(f32[2,8,5,128]{3,0,2,1:T(2,128)S(1)} %bitcast.25, f32[8]{0:T(128)S(1)} %multiply_divide_fusion.1), kind=kLoop, calls=%fused_computation.9 | loop fusion | flops 20480 | bytes 61472 | tf_op jit(solution)/shard_map/transpose | solution.py:461
  56.4 0.0 copy-done
  56.4 3.1 %convert_add_fusion = f32[2,2064,128]{2,1,0:T(8,128)} fusion(f32[2,2064,128]{2,1,0:T(8,128)} %get-tuple-element.10, bf16[2,2064,128]{2,1,0:T(8,128)(2,1)S(1)} %copy-done), kind=kLoop, calls=%fused_computation | loop fusion | flops 1056768 | bytes 5283840 | tf_op jit(solution)/shard_map/add | solution.py:454
  (8 shorter events, 0.2 us)
Async XLA Ops:
  1.8 3.5 %copy-start.3 = (s32[32]{0:T(128)S(1)}, s32[32]{0:T(128)}, u32[]{:S(2)}) copy-start(s32[32]{0:T(128)} %param.11) | copy-start | bytes 388
  1.8 5.5 %copy-start.2 = (bf16[192,2,2,128]{3,2,1,0:T(2,128)(2,1)S(1)}, bf16[192,2,2,128]{3,2,1,0:T(2,128)(2,1)}, u32[]{:S(2)}) copy-start(bf16[192,2,2,128]{3,2,1,0:T(2,128)(2,1)} %param.8) | copy-start | bytes 589828
  1.8 6.3 %copy-start.1 = (bf16[192,2,5,128]{3,1,2,0:T(2,128)(2,1)S(1)}, bf16[192,2,5,128]{3,1,2,0:T(2,128)(2,1)}, u32[]{:S(2)}) copy-start(bf16[192,2,5,128]{3,1,2,0:T(2,128)(2,1)} %param.7) | copy-start | bytes 1474564
  52.2 4.2 %copy-start = (bf16[2,2064,128]{2,1,0:T(8,128)(2,1)S(1)}, bf16[2,2064,128]{2,1,0:T(8,128)(2,1)}, u32[]{:S(2)}) copy-start(bf16[2,2064,128]{2,1,0:T(8,128)(2,1)} %prior.1) | copy-start | bytes 3170308

commit v2 on v1

--- a/solution.py
+++ b/solution.py
@@ -18,21 +18,23 @@
 
 
 def pick_kernel(ids_ref, query_table, pair_table, query_out, pair_out, query_sem, pair_sem):
-    step_count = query_out.shape[0]
-
-    def copies(step):
-        row = ids_ref[step]
-        return (
-            pltpu.make_async_copy(query_table.at[row], query_out.at[step], query_sem.at[step]),
-            pltpu.make_async_copy(pair_table.at[row], pair_out.at[step], pair_sem.at[step]),
-        )
-
-    for step in range(step_count):
-        for copy in copies(step):
-            copy.start()
-    for step in range(step_count):
-        for copy in copies(step):
-            copy.wait()
+    vocab_rows = query_table.shape[0]
+    first_row = lax.axis_index("ctx") * vocab_rows
+    query_out[...] = jnp.zeros_like(query_out)
+    pair_out[...] = jnp.zeros_like(pair_out)
+
+    def each(step, act):
+        row = ids_ref[step] - first_row
+
+        @pl.when(jnp.logical_and(row >= 0, row < vocab_rows))
+        def _():
+            act(pltpu.make_async_copy(query_table.at[row], query_out.at[step], query_sem.at[step]))
+            act(pltpu.make_async_copy(pair_table.at[row], pair_out.at[step], pair_sem.at[step]))
+
+    for step in range(query_out.shape[0]):
+        each(step, lambda copy: copy.start())
+    for step in range(query_out.shape[0]):
+        each(step, lambda copy: copy.wait())
 
 
 def pick_rows(ids, query_table, pair_table):
@@ -59,9 +61,13 @@
 
 def main_kernel(
     sizes,
+    counts,
     queries,
     blob,
     prior,
+    window_out,
+    step_out,
+    state_out,
     out,
     state,
     land_blob,
@@ -291,6 +297,17 @@
         prior_copy(prior.at[head], partner, head, 0, partner).wait_recv()
         carry(partner, head, 0, row_tiles)
 
+    def state_copy(head):
+        return pltpu.make_async_copy(state.at[head], state_out.at[head], local_sem.at[2 + head])
+
+    def positions(tile):
+        local = tile * TILE + lax.broadcasted_iota(jnp.int32, (TILE, 1), 0)
+        return jnp.where(
+            local < window_rows,
+            local + me * window_rows,
+            local - window_rows + window * group + me * (per_shard * group),
+        )
+
     first_offset, lead = place(me)
     for head in range(heads):
         keys_turned = transposed(key_rows[head])
@@ -317,15 +334,21 @@
             features = jnp.concatenate(pieces, axis=1)
             return jnp.dot(features, value_rows[head], preferred_element_type=jnp.float32)
 
+        def before(rows):
+            return prior[head, rows, :].astype(jnp.float32) if shifted else 0.0
+
         whole_blocks = state_rows // LANES
 
         @pl.loop(0, whole_blocks)
         def _(block):
-            state[head, pl.ds(pl.multiple_of(block * LANES, LANES), LANES), :] = state_block(block)
+            rows = pl.ds(pl.multiple_of(block * LANES, LANES), LANES)
+            state[head, rows, :] = before(rows) + state_block(block)
 
         rest = state_rows - whole_blocks * LANES
         if rest > 0:
-            state[head, pl.ds(whole_blocks * LANES, rest), :] = state_block(whole_blocks)[:rest]
+            rows = pl.ds(whole_blocks * LANES, rest)
+            state[head, rows, :] = before(rows) + state_block(whole_blocks)[:rest]
+        state_copy(head).start()
 
         @pl.loop(0, row_tiles)
         def _(tile):
@@ -336,12 +359,7 @@
                 contract_last,
                 preferred_element_type=jnp.float32,
             )
-            local = tile * TILE + lax.broadcasted_iota(jnp.int32, (TILE, 1), 0)
-            position = jnp.where(
-                local < window_rows,
-                local + me * window_rows,
-                local - window_rows + window * group + me * (per_shard * group),
-            )
+            position = positions(tile)
             key_index = lax.broadcasted_iota(jnp.int32, scores.shape, 1)
             allowed = position >= key_index * group
             weights = jnp.where(allowed, scores * scores, 0.0).astype(jnp.bfloat16)
@@ -360,7 +378,18 @@
 
     for head in range(heads):
         for tile in range(row_tiles):
-            out[head, pl.ds(tile * TILE, TILE), :] += total_turned[head, tile].T
+            first = tile * TILE
+            token = jnp.floor((positions(tile).astype(jnp.float32) + 0.5) / group)
+            place_in_prompt = token + (counts[0] + 1).astype(jnp.float32)
+            scale = 1.0 / (LANES * jnp.sqrt(place_in_prompt))
+            total = out[head, pl.ds(first, TILE), :] + total_turned[head, tile].T
+            total = (total * scale).astype(jnp.bfloat16)
+            split = min(max(window_rows - first, 0), TILE)
+            if split > 0:
+                window_out[head, pl.ds(first, split), :] = total[:split]
+            if split < TILE:
+                step_out[head, pl.ds(first + split - window_rows, TILE - split), :] = total[split:]
+        state_copy(head).wait()
 
     for slot in range(chips):
         blob_own(slot).wait_send()
@@ -372,8 +401,9 @@
             prior_forward(step, head).wait_send()
 
 
-def combine(sizes, queries, blob, prior, out_rows):
+def combine(sizes, counts, queries, blob, prior, out_rows):
     n, heads, group, tok_rows, step_count, rows_valid = sizes
+    window_rows = tok_rows * group
     lead = max(source * rows_valid % LANES for source in range(n))
     padded_rows = round_up(lead + rows_valid, LANES)
     chunks = out_rows // LANES
@@ -384,12 +414,15 @@
     return pl.pallas_call(
         functools.partial(main_kernel, sizes),
         out_shape=(
-            jax.ShapeDtypeStruct((heads, out_rows, LANES), jnp.float32),
+            jax.ShapeDtypeStruct((heads, window_rows, LANES), jnp.bfloat16),
+            jax.ShapeDtypeStruct((heads, out_rows - window_rows, LANES), jnp.bfloat16),
             jax.ShapeDtypeStruct((heads, state_rows, LANES), jnp.float32),
         ),
-        in_specs=[vmem] * 3,
-        out_specs=(vmem, vmem),
+        in_specs=[pl.BlockSpec(memory_space=pltpu.SMEM)] + [vmem] * 3,
+        out_specs=(vmem, vmem, pl.BlockSpec(memory_space=pl.ANY)),
         scratch_shapes=[
+            pltpu.VMEM((heads, out_rows, LANES), jnp.float32),
+            pltpu.VMEM((heads, state_rows, LANES), jnp.float32),
             pltpu.VMEM((n,) + blob.shape, jnp.bfloat16),
             pltpu.VMEM((n, heads, padded_rows, LANES), jnp.bfloat16),
             pltpu.VMEM((heads, out_rows, LANES), jnp.bfloat16),
@@ -405,13 +438,13 @@
             pltpu.SemaphoreType.DMA((n,)),
             pltpu.SemaphoreType.DMA((slots, heads)),
             pltpu.SemaphoreType.DMA((n, heads)),
-            pltpu.SemaphoreType.DMA((2,)),
+            pltpu.SemaphoreType.DMA((2 + heads,)),
         ],
         compiler_params=pltpu.CompilerParams(
             collective_id=0, has_side_effects=True, vmem_limit_bytes=56 * 2**20
         ),
         name="combine",
-    )(queries, blob, prior)
+    )(counts, queries, blob, prior)
 
 
 def on_device(queries, keys_values, prior_state, counts, continuation, query_table, pair_table):
@@ -422,14 +455,9 @@
     per_shard = step_count // n
     rows_valid = prior_state.shape[1]
 
-    vocab_rows = query_table.shape[0]
-    local_ids = continuation - shard_index * vocab_rows
-    inside = (local_ids >= 0) & (local_ids < vocab_rows)
-    safe_ids = jnp.clip(local_ids, 0, vocab_rows - 1)
-    query_pick, pair_pick = pick_rows(safe_ids, query_table.transpose(0, 2, 1, 3), pair_table)
-    mask = inside[:, None, None, None]
-    query_pick = jnp.where(mask, query_pick, jnp.zeros_like(query_pick))
-    pair_pick = jnp.where(mask, pair_pick, jnp.zeros_like(pair_pick))
+    query_pick, pair_pick = pick_rows(
+        continuation, query_table.transpose(0, 2, 1, 3), pair_table
+    )
 
     window_planes = keys_values.transpose(2, 1, 0, 3).reshape(2 * heads, tok_rows, head_size)
     step_planes = pair_pick.transpose(2, 1, 0, 3)
@@ -449,23 +477,14 @@
         )
     out_rows = round_up((tok_rows + per_shard) * group, TILE)
     sizes = (n, heads, group, tok_rows, step_count, rows_valid)
-    total, added = combine(sizes, query_planes, blob, prior, out_rows)
-
-    decode_state = prior_state.astype(jnp.float32) + added[:, :rows_valid]
-
-    def finish(rows, first_position):
-        count = rows.shape[1] // group
-        positions = first_position + jnp.arange(count, dtype=jnp.int32) + 1
-        scale = 1.0 / (head_size * jnp.sqrt(positions.astype(jnp.float32)))
-        rows = rows.reshape(heads, count, group, head_size) * scale[None, :, None, None]
-        return rows.astype(jnp.bfloat16).transpose(1, 0, 2, 3)
-
-    window_rows = tok_rows * group
-    readout = finish(total[:, :window_rows], counts[0] + shard_index * tok_rows)
-    decode_out = finish(
-        total[:, window_rows : window_rows + per_shard * group],
-        counts[0] + n * tok_rows + shard_index * per_shard,
-    )
+    window_out, step_out, state = combine(sizes, counts, query_planes, blob, prior, out_rows)
+
+    decode_state = state
+    if rows_valid % 16 != 0:
+        decode_state = prior_state.astype(jnp.float32) + state[:, :rows_valid]
+    readout = window_out.reshape(heads, tok_rows, group, head_size).transpose(1, 0, 2, 3)
+    decode_out = step_out[:, : per_shard * group]
+    decode_out = decode_out.reshape(heads, per_shard, group, head_size).transpose(1, 0, 2, 3)
     return (readout, decode_out, decode_state)
 
 

time: 60 us -> 56.2 us (0.937)
  other arithmetic: 8.85 us -> 0.74 us
  local copies, waits for them, and re-layouts: 3.8 us -> 9.32 us
  Pallas kernels: 45.5 us -> 44.3 us
    transpose x4 -> x0, other arithmetic: 3.81 us -> none  [the longest x2 1.9 us: finish(): return rows.astype(jnp.bfloat16).transpose(1, 0, 2, 3)]
    add x1 -> x0, other arithmetic: 3.09 us -> none  [on_device(): decode_state = prior_state.astype(jnp.float32) + added[:, :rows_valid]]
    unnamed x8 -> x5, local copies, waits for them, and re-layouts: 0.02 us -> 3.06 us
    pallas_call x0 -> x1, local copies, waits for them, and re-layouts: none -> 2.31 us  [combine(): pl.pallas_call(functools.partial(main_kernel, sizes), out_shape=(jax.Shap...]
    slice x4 -> x2, local copies, waits for them, and re-layouts: 2.84 us -> 1.35 us  [on_device(): decode_out = step_out[:, :per_shard * group]]
    min x1 -> x0, other arithmetic: 1.17 us -> none  [on_device(): safe_ids = jnp.clip(local_ids, 0, vocab_rows - 1)]
    transpose x1, local copies, waits for them, and re-layouts: 0.02 us -> 0.91 us  [on_device(): query_pick.transpose(2, 0, 1, 3)]
    transpose x1, local copies, waits for them, and re-layouts: 0.01 us -> 0.77 us  [on_device(): step_planes = pair_pick.transpose(2, 1, 0, 3)]
where the time goes in v2:
time: 56.2 us; the launch traced here: 55.7 us
  Pallas kernels  44.3 us (79%)
  local copies, waits for them, and re-layouts  9.32 us (17%)
  between operations  1.34 us (2%)
  other arithmetic  0.74 us (1%)
    pallas_call x1, Pallas kernels, combine(): pl.pallas_call(functools.partial(main_kernel, sizes), out_shape=(jax.Shap...  41.4 us
    unnamed x5, local copies, waits for them, and re-layouts  3.06 us
    pallas_call x1, Pallas kernels, pick_rows(): pl.pallas_call(pick_kernel, out_shape=(jax.ShapeDtypeStruct((steps,) + qu...  2.92 us
    pallas_call x1, local copies, waits for them, and re-layouts, combine(): pl.pallas_call(functools.partial(main_kernel, sizes), out_shape=(jax.Shap...  2.31 us
    slice x2, local copies, waits for them, and re-layouts, on_device(): decode_out = step_out[:, :per_shard * group]  1.35 us

profile of v2, /device:TPU:1, one launch (start us, length us, event | category | flops | bytes accessed | tf_op | source)
XLA Modules:
  0.0 55.7 jit_solution(14425136801567141967)
XLA Ops:
  1.3 0.0 copy-start.1
  1.3 0.0 copy-start
  1.3 2.9 %pick_rows.1 = (bf16[32,5,2,128]{3,2,1,0:T(2,128)(2,1)}, bf16[32,2,2,128]{3,2,1,0:T(2,128)(2,1)}) custom-call(s32[32]{0:T(128)} %ids_ref.1, bf16[18992,5,2,128]{3,2,1,0:T(2,128)(2,1)} %bitcast.15, bf16[18992,2,2,128]{3,2,1,0:T(2,128)(2,1)} %pair_table.1), custom_call_target="tpu_custom_call" | custom-call | tf_op jit(solution)/shard_map/pick_rows/pallas_call | solution.py:42
  4.2 0.8 %copy.17 = bf16[2,2,32,128]{3,2,1,0:T(8,128)(2,1)S(1)} copy(bf16[2,2,32,128]{3,0,1,2:T(2,128)(2,1)} %bitcast.22) | data formatting | bytes 65536 | tf_op jit(solution)/shard_map/transpose | solution.py:463
  5.0 0.9 %copy.18 = bf16[2,32,5,128]{3,2,1,0:T(8,128)(2,1)S(1)} copy(bf16[2,32,5,128]{3,0,2,1:T(2,128)(2,1)} %bitcast.21) | data formatting | bytes 163840 | tf_op jit(solution)/shard_map/transpose | solution.py:465
  5.9 0.0 copy-done.1
  6.0 0.7 %pad_maximum_fusion.blob = bf16[4,304,128]{2,1,0:T(8,128)(2,1)} fusion(bf16[4,80,128]{2,1,0:T(8,128)(2,1)S(1)} %reshape.27, bf16[4,32,128]{2,1,0:T(8,128)(2,1)S(1)} %bitcast.20, bf16[4,192,128]{2,1,0:T(8,128)(2,1)S(1)} %bitcast.16), kind=kLoop, calls=%fused_computation | loop fusion | flops 933888 | bytes 622592 | tf_op jit(solution)/shard_map/concatenate | solution.py:468
  6.7 0.0 copy-done
  6.7 0.8 %copy.19.queries = bf16[2,960,128]{2,1,0:T(8,128)(2,1)} copy(bf16[2,960,128]{2,0,1:T(2,128)(2,1)S(1)} %bitcast.17) | data formatting | bytes 983040 | tf_op jit(solution)/shard_map/reshape | solution.py:469
  7.6 41.4 %combine.1 = (bf16[2,960,128]{2,1,0:T(8,128)(2,1)}, bf16[2,64,128]{2,1,0:T(8,128)(2,1)}, f32[2,2064,128]{2,1,0:T(8,128)}) custom-call(s32[1]{0:T(128)S(6)} %copy.23.counts, bf16[2,960,128]{2,1,0:T(8,128)(2,1)} %copy.19.queries, bf16[4,304,128]{2,1,0:T(8,128)(2,1)} %pad_maximum_fusion.blob, bf16[2,2064,128]{2,1,0:T(8,128)(2,1)} %prior.1), custom_call_target="tpu_custom_call" | custom-call | tf_op jit(solution)/shard_map/combine/pallas_call | solution.py:414
  49.0 2.3 %copy.20 = bf16[2,960,128]{2,0,1:T(2,128)(2,1)} copy(bf16[2,960,128]{2,1,0:T(8,128)(2,1)} %get-tuple-element.10) | data formatting | bytes 983040 | tf_op jit(solution)/shard_map/combine/pallas_call | solution.py:414
  51.3 0.7 %slice.3 = bf16[2,40,128]{2,1,0:T(8,128)(2,1)S(1)} slice(bf16[2,64,128]{2,1,0:T(8,128)(2,1)} %get-tuple-element.11), slice={[0:2], [0:40], [0:128]} | slice | bytes 40960 | tf_op jit(solution)/shard_map/slice | solution.py:486
  52.1 0.6 %copy.21 = bf16[2,40,128]{2,0,1:T(2,128)(2,1)} copy(bf16[2,40,128]{2,1,0:T(8,128)(2,1)S(1)} %slice.3) | data formatting | bytes 40960 | tf_op jit(solution)/shard_map/slice | solution.py:486
  52.7 3.1 %copy.24 = f32[2,2064,128]{2,1,0:T(8,128)} copy(f32[2,2064,128]{2,1,0:T(8,128)} %get-tuple-element.18) | data formatting | bytes 4227072
  (2 shorter events, 0.1 us)
Async XLA Ops:
  1.3 4.7 %copy-start.1 = (bf16[192,2,2,128]{3,2,1,0:T(2,128)(2,1)S(1)}, bf16[192,2,2,128]{3,2,1,0:T(2,128)(2,1)}, u32[]{:S(2)}) copy-start(bf16[192,2,2,128]{3,2,1,0:T(2,128)(2,1)} %param.8) | copy-start | bytes 589828
  1.3 5.5 %copy-start = (bf16[192,2,5,128]{3,1,2,0:T(2,128)(2,1)S(1)}, bf16[192,2,5,128]{3,1,2,0:T(2,128)(2,1)}, u32[]{:S(2)}) copy-start(bf16[192,2,5,128]{3,1,2,0:T(2,128)(2,1)} %param.7) | copy-start | bytes 1474564

commit v3 on v2

--- a/solution.py
+++ b/solution.py
@@ -253,11 +253,18 @@
         turn_queries(head, 0, full_tiles)
         carry(me, head, 0, full_tiles)
 
+    def carry_partner(head):
+        prior_copy(prior.at[head], partner, head, 0, partner).wait_recv()
+        carry(partner, head, 0, full_tiles)
+
+    carry_partner(0)
     own_blob.wait()
     blob_copy(blob, partner, 0, partner).wait_recv()
     for step in range(1, chips):
         blob_copy(blob, across(step), 0, partner).wait_recv()
         blob_forward(step).start()
+    for head in range(1, heads):
+        carry_partner(head)
     for step in range(1, chips):
         blob_copy(blob, twin(across(step)), 0, partner).wait_recv()
 
@@ -294,8 +301,7 @@
 
     for head in range(heads):
         carry(me, head, full_tiles, row_tiles)
-        prior_copy(prior.at[head], partner, head, 0, partner).wait_recv()
-        carry(partner, head, 0, row_tiles)
+        carry(partner, head, full_tiles, row_tiles)
 
     def state_copy(head):
         return pltpu.make_async_copy(state.at[head], state_out.at[head], local_sem.at[2 + head])
@@ -367,11 +373,13 @@
                 weights, value_rows[head], preferred_element_type=jnp.float32
             )
 
+        for step in range(1, chips):
+            prior_copy(prior.at[head], across(step), head, 0, partner).wait_recv()
+            prior_forward(step, head).start()
+
     for step in range(1, chips):
         source = across(step)
         for head in range(heads):
-            prior_copy(prior.at[head], source, head, 0, partner).wait_recv()
-            prior_forward(step, head).start()
             carry(source, head, 0, row_tiles)
             prior_copy(prior.at[head], twin(source), head, 0, partner).wait_recv()
             carry(twin(source), head, 0, row_tiles)

time: 56.2 us -> 59.2 us (1.053)
  Pallas kernels: 44.3 us -> 46.8 us
    pallas_call x1, Pallas kernels: 41.4 us -> 43.8 us  [combine(): pl.pallas_call(functools.partial(main_kernel, sizes), out_shape=(jax.Shap...]
where the time goes in v3:
time: 59.2 us; the launch traced here: 58.2 us
  Pallas kernels  46.8 us (79%)
  local copies, waits for them, and re-layouts  9.32 us (16%)
  between operations  1.34 us (2%)
  other arithmetic  0.74 us (1%)
    pallas_call x1, Pallas kernels, combine(): pl.pallas_call(functools.partial(main_kernel, sizes), out_shape=(jax.Shap...  43.8 us
    unnamed x5, local copies, waits for them, and re-layouts  3.06 us
    pallas_call x1, Pallas kernels, pick_rows(): pl.pallas_call(pick_kernel, out_shape=(jax.ShapeDtypeStruct((steps,) + qu...  2.99 us
    pallas_call x1, local copies, waits for them, and re-layouts, combine(): pl.pallas_call(functools.partial(main_kernel, sizes), out_shape=(jax.Shap...  2.31 us
    slice x2, local copies, waits for them, and re-layouts, on_device(): decode_out = step_out[:, :per_shard * group]  1.35 us

profile of v3, /device:TPU:1, one launch (start us, length us, event | category | flops | bytes accessed | tf_op | source)
XLA Modules:
  0.0 58.2 jit_solution(583336092506238054)
XLA Ops:
  1.3 0.0 copy-start.1
  1.3 0.0 copy-start
  1.3 3.0 %pick_rows.1 = (bf16[32,5,2,128]{3,2,1,0:T(2,128)(2,1)}, bf16[32,2,2,128]{3,2,1,0:T(2,128)(2,1)}) custom-call(s32[32]{0:T(128)} %ids_ref.1, bf16[18992,5,2,128]{3,2,1,0:T(2,128)(2,1)} %bitcast.15, bf16[18992,2,2,128]{3,2,1,0:T(2,128)(2,1)} %pair_table.1), custom_call_target="tpu_custom_call" | custom-call | tf_op jit(solution)/shard_map/pick_rows/pallas_call | solution.py:42
  4.3 0.8 %copy.17 = bf16[2,2,32,128]{3,2,1,0:T(8,128)(2,1)S(1)} copy(bf16[2,2,32,128]{3,0,1,2:T(2,128)(2,1)} %bitcast.22) | data formatting | bytes 65536 | tf_op jit(solution)/shard_map/transpose | solution.py:471
  5.1 0.9 %copy.18 = bf16[2,32,5,128]{3,2,1,0:T(8,128)(2,1)S(1)} copy(bf16[2,32,5,128]{3,0,2,1:T(2,128)(2,1)} %bitcast.21) | data formatting | bytes 163840 | tf_op jit(solution)/shard_map/transpose | solution.py:473
  6.0 0.0 copy-done.1
  6.1 0.7 %pad_maximum_fusion.blob = bf16[4,304,128]{2,1,0:T(8,128)(2,1)} fusion(bf16[4,80,128]{2,1,0:T(8,128)(2,1)S(1)} %reshape.27, bf16[4,32,128]{2,1,0:T(8,128)(2,1)S(1)} %bitcast.20, bf16[4,192,128]{2,1,0:T(8,128)(2,1)S(1)} %bitcast.16), kind=kLoop, calls=%fused_computation | loop fusion | flops 933888 | bytes 622592 | tf_op jit(solution)/shard_map/concatenate | solution.py:476
  6.8 0.0 copy-done
  6.8 0.8 %copy.19.queries = bf16[2,960,128]{2,1,0:T(8,128)(2,1)} copy(bf16[2,960,128]{2,0,1:T(2,128)(2,1)S(1)} %bitcast.17) | data formatting | bytes 983040 | tf_op jit(solution)/shard_map/reshape | solution.py:477
  7.7 43.8 %combine.1 = (bf16[2,960,128]{2,1,0:T(8,128)(2,1)}, bf16[2,64,128]{2,1,0:T(8,128)(2,1)}, f32[2,2064,128]{2,1,0:T(8,128)}) custom-call(s32[1]{0:T(128)S(6)} %copy.23.counts, bf16[2,960,128]{2,1,0:T(8,128)(2,1)} %copy.19.queries, bf16[4,304,128]{2,1,0:T(8,128)(2,1)} %pad_maximum_fusion.blob, bf16[2,2064,128]{2,1,0:T(8,128)(2,1)} %prior.1), custom_call_target="tpu_custom_call" | custom-call | tf_op jit(solution)/shard_map/combine/pallas_call | solution.py:422
  51.4 2.3 %copy.20 = bf16[2,960,128]{2,0,1:T(2,128)(2,1)} copy(bf16[2,960,128]{2,1,0:T(8,128)(2,1)} %get-tuple-element.10) | data formatting | bytes 983040 | tf_op jit(solution)/shard_map/combine/pallas_call | solution.py:422
  53.8 0.7 %slice.3 = bf16[2,40,128]{2,1,0:T(8,128)(2,1)S(1)} slice(bf16[2,64,128]{2,1,0:T(8,128)(2,1)} %get-tuple-element.11), slice={[0:2], [0:40], [0:128]} | slice | bytes 40960 | tf_op jit(solution)/shard_map/slice | solution.py:494
  54.5 0.6 %copy.21 = bf16[2,40,128]{2,0,1:T(2,128)(2,1)} copy(bf16[2,40,128]{2,1,0:T(8,128)(2,1)S(1)} %slice.3) | data formatting | bytes 40960 | tf_op jit(solution)/shard_map/slice | solution.py:494
  55.1 3.1 %copy.24 = f32[2,2064,128]{2,1,0:T(8,128)} copy(f32[2,2064,128]{2,1,0:T(8,128)} %get-tuple-element.18) | data formatting | bytes 4227072
  (2 shorter events, 0.1 us)
Async XLA Ops:
  1.3 4.8 %copy-start.1 = (bf16[192,2,2,128]{3,2,1,0:T(2,128)(2,1)S(1)}, bf16[192,2,2,128]{3,2,1,0:T(2,128)(2,1)}, u32[]{:S(2)}) copy-start(bf16[192,2,2,128]{3,2,1,0:T(2,128)(2,1)} %param.8) | copy-start | bytes 589828
  1.3 5.5 %copy-start = (bf16[192,2,5,128]{3,1,2,0:T(2,128)(2,1)S(1)}, bf16[192,2,5,128]{3,1,2,0:T(2,128)(2,1)}, u32[]{:S(2)}) copy-start(bf16[192,2,5,128]{3,1,2,0:T(2,128)(2,1)} %param.7) | copy-start | bytes 1474564
